TPU v7x, 512 devices: a whole 4x8x8 slice. The times are simulated.
512 devices in a mesh: section: 16 (over x_lo, z), dp: 32 (over x_hi, y, core).
Axes of the slice: x: 4 (x_hi: 2, x_lo: 2; x = x_hi * 2 + x_lo), y: 8, z: 8, core: 2. Of those that a mesh axis runs over, the one named last changes fastest.
Arguments:
- act_in: float32 [16, 2, 32, 15, 15, 256], P('section', None, 'dp'), may hold values from -6 to 6
- act_mid: float32 [16, 2, 32, 15, 15, 256], P('section', None, 'dp'), may hold values from 0 to 2
- relu_mask: int32 [16, 2, 32, 15, 15, 256], P('section', None, 'dp'), may hold values 0 or 1
- arriving: float32 [16, 32, 15, 15, 256], P('section', 'dp'), may hold values from -6 to 6
- loss_grad: float32 [1, 32, 15, 15, 256], P(None, 'dp'), may hold values from -6 to 6
- w_first: float32 [16, 1792, 256], P('section', 'dp'), may hold values from -0.125 to 0.125
- w_second: float32 [16, 1792, 256], P('section', 'dp'), may hold values from -0.125 to 0.125
Outputs:
- data_grad: float32 [16, 2, 32, 15, 15, 256], P('section', None, 'dp')
- first_grad: float32 [16, 1792, 256], P('section', 'dp')
- second_grad: float32 [16, 1792, 256], P('section', 'dp')
All inputs are finite; a program needn't handle non-finite values. No bound on the sum of `relu_mask` on one device may be relied on, other than what follows from the above.
Results may differ from a plain program's by a relative error of at most 0.00011.
Values sent between devices are 32-bit elements; how exact they have to be, the bound alone decides.
A program may use at most 64 MiB of HBM per device.

v0:
```python
import jax
import jax.numpy as jnp
from jax import lax
from jax.sharding import PartitionSpec as P


def shifted(shard, axis, by):
    peers = lax.axis_size(axis)
    pairs = [(i, i + by) for i in range(peers) if 0 <= i + by < peers]
    return lax.ppermute(shard, axis, pairs)


def spread_taps(values, spatial):
    widths = [(0, 0)] * 4
    widths[spatial] = (3, 3)
    padded = jnp.pad(values, widths)
    extent = values.shape[spatial]
    pieces = [
        lax.slice_in_dim(padded, offset, offset + extent, axis=spatial) for offset in range(7)
    ]
    return jnp.concatenate(pieces, axis=-1)


def fold_taps(products, spatial):
    channels = products.shape[-1] // 7
    widths = [(0, 0)] * 4
    widths[spatial] = (3, 3)
    padded = jnp.pad(products, widths)
    extent = products.shape[spatial]
    summed = jnp.zeros(products.shape[:-1] + (channels,), products.dtype)
    for offset in range(7):
        window = lax.slice_in_dim(padded, 6 - offset, 6 - offset + extent, axis=spatial)
        summed = summed + window[..., offset * channels : (offset + 1) * channels]
    return summed


def project_taps(values, weight):
    return jnp.einsum("nhwc,kc->nhwk", values, weight, precision=lax.Precision.HIGHEST)


def flat_patches(values, spatial):
    patches = spread_taps(values.reshape((-1,) + values.shape[2:]), spatial)
    return patches.reshape(-1, patches.shape[-1])


def correlate(patches, grad_rows, mean_scale):
    return jnp.einsum("rk,rc->kc", patches, grad_rows, precision=lax.Precision.HIGHEST) * mean_scale


def local(act_in, act_mid, relu_mask, arriving, loss_grad, w_first, w_second):
    tick_count = act_in.shape[1]
    channels = act_in.shape[-1]
    is_last = lax.axis_index("section") == lax.axis_size("section") - 1
    full_first, full_second = (
        lax.all_gather(w_first[0], "dp", axis=0, tiled=True),
        lax.all_gather(w_second[0], "dp", axis=0, tiled=True),
    )
    incoming = arriving[0]
    mid_grad = fold_taps(project_taps(incoming, full_second), 1)
    in_list = [incoming]
    pre_list = []
    out_list = []
    for tick_index in range(tick_count):
        if tick_index > 0:
            from_above = shifted(out_list[-1], "section", -1)
            incoming = jnp.where(is_last, loss_grad[tick_index - 1], from_above)
            in_list.append(incoming)
            mid_grad = fold_taps(project_taps(incoming, full_second), 1)
        pre_grad = mid_grad * relu_mask[0, tick_index].astype(jnp.float32)
        out_list.append(fold_taps(project_taps(pre_grad, full_first), 2))
        pre_list.append(pre_grad)
    data_grad = jnp.stack(out_list, axis=0)[None]
    mean_scale = 1.0 / (tick_count * act_in.shape[2] * lax.axis_size("dp"))
    first_patches = flat_patches(act_in[0], 2)
    second_patches = flat_patches(act_mid[0], 1)
    pre_rows = jnp.stack(pre_list, axis=0).reshape(-1, channels)
    in_rows = jnp.stack(in_list, axis=0).reshape(-1, channels)
    summed = lax.psum_scatter(
        jnp.concatenate(
            [
                correlate(first_patches, pre_rows, mean_scale),
                correlate(second_patches, in_rows, mean_scale),
            ],
            axis=1,
        ),
        "dp",
        scatter_dimension=0,
        tiled=True,
    )
    first_grad = summed[:, :channels]
    second_grad = summed[:, channels:]
    return (data_grad, first_grad[None], second_grad[None])


def solution(mesh):
    return jax.shard_map(
        local,
        mesh=mesh,
        in_specs=(
            P("section", None, "dp", None, None, None),
            P("section", None, "dp", None, None, None),
            P("section", None, "dp", None, None, None),
            P("section", "dp", None, None, None),
            P(None, "dp", None, None, None),
            P("section", "dp", None),
            P("section", "dp", None),
        ),
        out_specs=(
            P("section", None, "dp", None, None, None),
            P("section", "dp", None),
            P("section", "dp", None),
        ),
        check_vma=False,
    )
```

profile of v0, /device:TPU:16, one launch (start us, length us, event | category | flops | bytes accessed | tf_op | source)
XLA Modules:
  0.0 363.2 jit_solution(2133980787343362848)
XLA Ops:
  8.7 1.3 copy.89
  10.0 2.1 reduce.1
  12.1 2.0 copy.90
  14.1 2.1 reduce
  16.3 1.7 pad_slice_fusion.24
  18.5 1.1 copy.52
  19.6 0.8 concatenate.52
  20.4 1.1 copy.53
  21.5 0.9 concatenate.53
  22.4 1.6 copy.54
  24.0 4.0 %pad_slice_fusion.30 = (f32[2,15,15,256]{3,0,2,1:T(2,128)}, f32[2,15,15,256]{3,0,2,1:T(2,128)}, f32[2,15,15,256]{3,0,2,1:T(2,128)}, f32[2,15,15,256]{3,0,2,1:T(2...) fusion(f32[2,15,15,256]{3,0,2,1:T(2,128)} %bitcast.66), kind=kLoop, calls=%fused_computation.46 | loop fusion | bytes 3225600 | tf_op jit(solution)/shard_map/slice | solution.py:19
  28.1 0.8 concatenate.39
  29.0 1.1 copy.42
  30.9 1.1 copy.43
  32.8 0.9 concatenate.42
  33.6 1.1 copy.44
  34.7 0.9 concatenate.43
  35.6 1.1 copy.45
  37.6 0.8 concatenate.45
  39.2 1.9 constant_dynamic-update-slice_fusion.6
  41.2 0.8 constant_dynamic-update-slice_fusion.12
  42.0 0.9 constant_dynamic-update-slice_fusion.11
  42.9 0.8 constant_dynamic-update-slice_fusion.10
  43.7 0.9 constant_dynamic-update-slice_fusion.9
  46.2 0.8 constant_dynamic-update-slice_fusion.5
  47.1 0.8 constant_dynamic-update-slice_fusion.4
  47.9 0.8 constant_dynamic-update-slice_fusion.3
  48.7 0.8 constant_dynamic-update-slice_fusion.2
  49.6 1.0 fusion.39
  50.6 48.9 %all-gather.5.cloned.1.call-done = f32[1,1792,256]{2,1,0:T(8,128)} async-done(((f32[1,56,256]{2,1,0:T(8,128)}), f32[1,1792,256]{2,1,0:T(8,128)}) %all-gather.5.cloned.1.call-update) | async-done | bytes 1835024 | tf_op jit(solution)/shard_map/all_gather | solution.py:56
  99.5 3.2 convolution_bitcast_fusion.3
  102.8 81.2 %all-gather.7.cloned.1.call-done = f32[1,1792,256]{2,1,0:T(8,128)} async-done(((f32[1,56,256]{2,1,0:T(8,128)}), f32[1,1792,256]{2,1,0:T(8,128)}) %all-gather.7.cloned.1.call-update) | async-done | bytes 1835024 | tf_op jit(solution)/shard_map/all_gather | solution.py:55
  184.1 3.3 convolution_bitcast_fusion.2
  187.6 1.6 collective-permute-start
  189.2 0.8 constant_dynamic-update-slice_fusion.1
  190.0 0.8 constant_dynamic-update-slice_fusion
  190.9 6.8 %collective-permute-done = f32[1,15,15,256]{3,2,1,0:T(8,128)S(1)} collective-permute-done((f32[1,15,15,256]{3,2,1,0:T(8,128)S(1)}, f32[1,15,15,256]{3,2,1,0:T(8,128)S(1)}, u32[]{:S(2)}, u32[]{:S(2)}) %collective-permute-start) | collective-permute-done | bytes 230432 | tf_op jit(solution)/shard_map/ppermute | solution.py:10
  199.2 1.9 reshape.78
  201.1 2.8 convolution_bitcast_fusion.1
  204.9 5.2 %convolution_multiply_fusion = f32[1792,256]{0,1:T(8,128)S(1)} fusion(f32[450,1792]{1,0:T(8,128)} %constant_dynamic-update-slice_fusion.7, f32[450,256]{1,0:T(8,128)S(1)} %copy-done.13), kind=kOutput, calls=%fused_computation.25 | convolution fusion | flops 2477719552 | bytes 5521408 | tf_op jit(solution)/shard_map/rk,rc->kc/dot_general | solution.py:47
  210.0 5.3 %convolution_multiply_fusion.1 = f32[1792,256]{0,1:T(8,128)S(1)} fusion(f32[450,1792]{1,0:T(8,128)} %constant_dynamic-update-slice_fusion, f32[450,256]{1,0:T(8,128)S(1)} %reshape.77), kind=kOutput, calls=%fused_computation.26 | convolution fusion | flops 2477719552 | bytes 5521408 | tf_op jit(solution)/shard_map/rk,rc->kc/dot_general | solution.py:47
  215.3 2.1 pad_maximum_fusion
  217.4 5.2 %copy.58 = f32[1792,512]{1,0:T(8,128)} copy(f32[1792,512]{0,1:T(8,128)} %pad_maximum_fusion) | data formatting | bytes 7340032
  222.8 1.3 copy-done
  224.1 2.6 convolution_bitcast_fusion
  226.9 1.2 copy.55
  228.2 126.0 %reduce-scatter.4.cloned.1.call-done = f32[56,512]{1,0:T(8,128)} async-done(((f32[1792,512]{1,0:T(8,128)}), f32[56,512]{1,0:T(8,128)}) %reduce-scatter.4.cloned.1.call-update) | async-done | bytes 114704
  354.2 0.9 fusion.40
  (78 shorter events, 11.9 us)
Async XLA Ops:
  7.2 92.3 %all-gather.5.cloned.1.call-start = ((), (), s32[]{:S(2)}) async-start(), calls=%async_computation.1 | async-start | bytes 1892352 | tf_op jit(solution)/shard_map/all_gather | solution.py:56
  7.9 176.2 %all-gather.7.cloned.1.call-start = ((), (), s32[]{:S(2)}) async-start(), calls=%async_computation.2 | async-start | bytes 1892352 | tf_op jit(solution)/shard_map/all_gather | solution.py:55
  8.6 345.5 %reduce-scatter.4.cloned.1.call-start = ((), (), s32[]{:S(2)}) async-start(), calls=%async_computation.3 | async-start | bytes 3784704
  32.8 4.7 %copy-start.14 = (f32[2,15,15,256]{3,0,2,1:T(2,128)S(1)}, f32[2,15,15,256]{3,0,2,1:T(2,128)}, u32[]{:S(2)}) copy-start(f32[2,15,15,256]{3,0,2,1:T(2,128)} %get-tuple-element.12) | copy-start | bytes 1382404
  37.5 7.0 %copy-start.6 = (f32[450,256]{1,0:T(8,128)S(1)}, f32[450,256]{1,0:T(8,128)}, u32[]{:S(2)}) copy-start(f32[450,256]{1,0:T(8,128)} %concatenate.52) | copy-start | bytes 1382404
  38.4 7.0 %copy-start.8 = (f32[450,256]{1,0:T(8,128)S(1)}, f32[450,256]{1,0:T(8,128)}, u32[]{:S(2)}) copy-start(f32[450,256]{1,0:T(8,128)} %concatenate.53) | copy-start | bytes 1382404
  39.2 7.0 %copy-start.9 = (f32[450,256]{1,0:T(8,128)S(1)}, f32[450,256]{1,0:T(8,128)}, u32[]{:S(2)}) copy-start(f32[450,256]{1,0:T(8,128)} %concatenate.40) | copy-start | bytes 1382404
  41.2 5.9 %copy-start.11 = (f32[450,256]{1,0:T(8,128)S(1)}, f32[450,256]{1,0:T(8,128)}, u32[]{:S(2)}) copy-start(f32[450,256]{1,0:T(8,128)} %concatenate.41) | copy-start | bytes 1382404
  42.0 5.9 %copy-start.10 = (f32[450,256]{1,0:T(8,128)S(1)}, f32[450,256]{1,0:T(8,128)}, u32[]{:S(2)}) copy-start(f32[450,256]{1,0:T(8,128)} %concatenate.42) | copy-start | bytes 1382404
  42.9 5.9 %copy-start.12 = (f32[450,256]{1,0:T(8,128)S(1)}, f32[450,256]{1,0:T(8,128)}, u32[]{:S(2)}) copy-start(f32[450,256]{1,0:T(8,128)} %concatenate.43) | copy-start | bytes 1382404
  43.7 5.9 %copy-start.20 = (s32[1,2,1,15,15,256]{5,2,4,3,1,0:T(1,128)S(1)}, s32[1,2,1,15,15,256]{5,2,4,3,1,0:T(1,128)}, u32[]{:S(2)}) copy-start(s32[1,2,1,15,15,256]{5,2,4,3,1,0:T(1,128)} %param.9) | copy-start | bytes 1382404
  44.6 54.9 %copy-start.16 = (f32[1,1,15,15,256]{4,1,3,2,0:T(1,128)S(1)}, f32[1,1,15,15,256]{4,1,3,2,0:T(1,128)}, u32[]{:S(2)}) copy-start(f32[1,1,15,15,256]{4,1,3,2,0:T(1,128)} %param.10) | copy-start | bytes 691204
  102.8 81.3 %copy-start.2 = (f32[1,15,15,256]{3,2,1,0:T(8,128)}, f32[1,15,15,256]{3,2,1,0:T(8,128)S(1)}, u32[]{:S(2)}) copy-start(f32[1,15,15,256]{3,2,1,0:T(8,128)S(1)} %fusion.10) | copy-start | bytes 691204
  184.1 5.1 %copy-start.5 = (f32[450,256]{1,0:T(8,128)S(1)}, f32[450,256]{1,0:T(8,128)}, u32[]{:S(2)}) copy-start(f32[450,256]{1,0:T(8,128)} %concatenate.44) | copy-start | bytes 1382404
  184.1 5.9 %copy-start.7 = (f32[450,256]{1,0:T(8,128)S(1)}, f32[450,256]{1,0:T(8,128)}, u32[]{:S(2)}) copy-start(f32[450,256]{1,0:T(8,128)} %concatenate.45) | copy-start | bytes 1382404
  184.1 13.6 %copy-start.15 = (f32[1,1,15,15,256]{4,1,3,2,0:T(1,128)S(1)}, f32[1,1,15,15,256]{4,1,3,2,0:T(1,128)}, u32[]{:S(2)}) copy-start(f32[1,1,15,15,256]{4,1,3,2,0:T(1,128)} %param.11) | copy-start | bytes 691204
  187.4 11.0 %copy-start.18 = (f32[1,1,15,15,256]{4,3,2,1,0:T(8,128)S(1)}, f32[1,1,15,15,256]{4,3,2,1,0:T(8,128)}, u32[]{:S(2)}) copy-start(f32[1,1,15,15,256]{4,3,2,1,0:T(8,128)} %copy.54) | copy-start | bytes 691204
  187.4 13.7 %copy-start.1 = (f32[1,1792,256]{2,1,0:T(8,128)S(1)}, f32[1,1792,256]{2,1,0:T(8,128)}, u32[]{:S(2)}) copy-start(f32[1,1792,256]{2,1,0:T(8,128)} %all-gather.5.cloned.1.call-done) | copy-start | bytes 5505028
  187.6 10.1 %collective-permute-start = (f32[1,15,15,256]{3,2,1,0:T(8,128)S(1)}, f32[1,15,15,256]{3,2,1,0:T(8,128)S(1)}, u32[]{:S(2)}, u32[]{:S(2)}) collective-permute-start(f32[1,15,15,256]{3,2,1,0:T(8,128)S(1)} %fusion.23), channel_id=1, source_target_pairs={{32,0},{64,32},{96,64},{128,96},{160,128},{192,160},{224,192},{256... | collective-permute-start | bytes 691208 | tf_op jit(solution)/shard_map/ppermute | solution.py:10
  197.7 0.7 copy-start.17
  201.1 2.8 copy-start.19
  201.1 3.6 %copy-start.3 = (f32[1,15,15,256]{3,2,1,0:T(8,128)S(1)}, f32[1,15,15,256]{3,2,1,0:T(8,128)}, u32[]{:S(2)}) copy-start(f32[1,15,15,256]{3,2,1,0:T(8,128)} %copy-done.2) | copy-start | bytes 691204
  203.9 1.0 copy-start.13
  204.0 0.7 copy-start.4
  222.6 1.5 copy-start
Sparse Core Ops, SparseCore 0:
  11.3 88.1 all-gather.4
  102.8 81.1 all-gather.6
  222.7 131.3 reduce-scatter.3
where the time goes:
time: 364 us; the launch traced here: 363 us
  waiting for transfers between devices  264 us (73%)
  local copies, waits for them, and re-layouts  52.7 us (14%)
  matrix products  22.3 us (6%)
  between operations  14.1 us (4%)
  other arithmetic  8.07 us (2%)
    unnamed x4, waiting for transfers between devices  127 us
    all_gather x1, waiting for transfers between devices, local(): lax.all_gather(w_first[0], 'dp', axis=0, tiled=True)  81.2 us
    all_gather x1, waiting for transfers between devices, local(): lax.all_gather(w_second[0], 'dp', axis=0, tiled=True)  48.9 us
    unnamed x63, local copies, waits for them, and re-layouts  26.9 us
    slice x14, local copies, waits for them, and re-layouts, spread_taps(): lax.slice_in_dim(padded, offset, offset + extent, axis=spatial)  12.5 us
    dot_general x4, matrix products, project_taps(): jnp.einsum('nhwc,kc->nhwk', values, weight, precision=lax.Precision.HIGHEST)  11.9 us
    dot_general x2, matrix products, correlate(): jnp.einsum('rk,rc->kc', patches, grad_rows, precision=lax.Precision.HIGHEST)  10.4 us
    concatenate x16, local copies, waits for them, and re-layouts, spread_taps(): return jnp.concatenate(pieces, axis=-1)  9.53 us
  transfers between devices with their start and end apart: 4, of which 4 were waited for; matrix products, arithmetic and copies ran while one was open for 14% of the time, Pallas kernels for 0%

commit v1 on v0

v1 whole, which is shorter than its diff:
```python
import functools

import jax
import jax.numpy as jnp
from jax import lax
from jax.experimental import pallas as pl
from jax.experimental.pallas import tpu as pltpu
from jax.sharding import PartitionSpec as P

MESH = pl.DeviceIdType.MESH
F32, BF16 = jnp.float32, jnp.bfloat16
PITCH = 16


def split(value):
    high = value.astype(BF16)
    return high, (value - high.astype(F32)).astype(BF16)


def dot_nt(a, b):
    return lax.dot_general(a, b, (((1,), (1,)), ((), ())), preferred_element_type=F32)


def dot_nn(a, b):
    return lax.dot_general(a, b, (((1,), (0,)), ((), ())), preferred_element_type=F32)


def kernel(
    sections,
    replicas,
    act_in,
    act_mid,
    relu_mask,
    arriving,
    loss_grad,
    w_first,
    w_second,
    data_grad,
    first_grad,
    second_grad,
    acts,
    masks,
    ups,
    act_t,
    rows_hi,
    rows_lo,
    cols_hi,
    cols_lo,
    weights,
    w_hi,
    w_lo,
    total,
    passed,
    above,
    out_map,
    grads,
    pair_in,
    ring_in,
    cross_in,
    grad_out,
    load_sem,
    own_sem,
    gather_send,
    gather_ring,
    gather_pair,
    shift_sem,
    reduce_send,
    reduce_pair,
    reduce_ring,
    reduce_cross,
    store_sem,
):
    ny = replicas // 4
    half = ny // 2
    shard, chans = w_first.shape[1:]
    height, width = act_in.shape[3:5]
    rows = height * PITCH
    taps = 7
    sec = lax.axis_index("section")
    dp = lax.axis_index("dp")
    x, y, c = dp // (2 * ny), (dp // 2) % ny, dp % 2

    def device(xr, rel, other):
        xx = 1 - x if xr else x
        cc = 1 - c if other else c
        return xx * (2 * ny) + lax.rem(y + rel + ny, ny) * 2 + cc

    def block(xr, rel, other=False):
        return pl.ds(pl.multiple_of(device(xr, rel, other) * shard, 8), shard)

    def slot(xr, rel):
        return xr * ny + rel % ny

    pair = {"dp": device(0, 0, True)}
    cross = {"dp": device(1, 0, False)}
    ahead = {1: {"dp": device(0, 1, False)}, -1: {"dp": device(0, -1, False)}}
    prev_section = {"section": lax.rem(sec + sections - 1, sections)}
    next_section = {"section": lax.rem(sec + 1, sections)}

    loads = []
    for t in range(2):
        loads.append((arriving.at[0, 0] if t == 0 else loss_grad.at[0, 0], ups.at[t]))
    for t in range(2):
        loads.append((act_mid.at[0, t, 0], acts.at[0, t]))
    for t in range(2):
        loads.append((relu_mask.at[0, t, 0], masks.at[t]))
    for t in range(2):
        loads.append((act_in.at[0, t, 0], acts.at[1, t]))
    loads = [pltpu.make_async_copy(s, d, load_sem.at[i]) for i, (s, d) in enumerate(loads)]
    for copy in loads:
        copy.start()
    shards = (w_second.at[0], w_first.at[0])
    own = [
        pltpu.make_async_copy(shards[w], weights.at[w, block(0, 0)], own_sem.at[w])
        for w in range(2)
    ]
    for copy in own:
        copy.start()

    barrier = pltpu.get_barrier_semaphore()
    friends = (pair, cross, ahead[1], ahead[-1], prev_section, next_section)
    for friend in friends:
        pl.semaphore_signal(barrier, inc=1, device_id=friend, device_id_type=MESH)
    pl.semaphore_wait(barrier, len(friends))

    def gather_copy(w, src, xr, rel, other, sem, to):
        return pltpu.make_async_remote_copy(
            src_ref=src,
            dst_ref=weights.at[w, block(xr, rel, other)],
            send_sem=gather_send.at[w],
            recv_sem=sem,
            device_id=to,
            device_id_type=MESH,
        )

    def gather_start(w):
        src = shards[w]
        for way in (1, -1):
            gather_copy(w, src, 0, 0, False, gather_ring.at[w, slot(0, -way)], ahead[way]).start()
        gather_copy(w, src, 0, 0, False, gather_ring.at[w, slot(1, 0)], cross).start()
        gather_copy(w, src, 0, 0, False, gather_pair.at[w, slot(0, 0)], pair).start()

    def gather_arrival(w, way, xr, hop):
        rel = -way * hop
        here = weights.at[w, block(xr, rel)]
        gather_copy(w, here, xr, rel, False, gather_ring.at[w, slot(xr, rel)], cross).wait_recv()
        ways = (1, -1) if hop == 0 else (way,)
        for onward in ways:
            last = hop + 1 == half
            if hop + 1 < half or (last and xr == (0 if onward == 1 else 1)):
                sem = gather_ring.at[w, slot(xr, rel - onward)]
                gather_copy(w, here, xr, rel, False, sem, ahead[onward]).start()
        gather_copy(w, here, xr, rel, False, gather_pair.at[w, slot(xr, rel)], pair).start()

    def gather_hop(hop):
        for xr in (0, 1):
            for w in range(2):
                if hop == 1 and xr == 1:
                    gather_arrival(w, 1, 1, 0)
            for w in range(2):
                for way in (1, -1):
                    if hop < half:
                        gather_arrival(w, way, xr, hop)

    def gather_end(w):
        gather_arrival(w, 1, 0, half)
        gather_arrival(w, -1, 1, half)

    def gather_pair_wait(w):
        own[w].wait()
        for xr in (0, 1):
            for rel in range(ny):
                here = weights.at[w, block(xr, rel, True)]
                sem = gather_pair.at[w, slot(xr, rel)]
                gather_copy(w, here, xr, rel, True, sem, pair).wait_recv()

    def round_weights(w):
        high, low = split(weights[w])
        w_hi[w] = high
        w_lo[w] = low

    top = 3 * PITCH

    def set_rows(t, value):
        high, low = split(value)
        rows_hi[t, top : top + rows] = high
        rows_lo[t, top : top + rows] = low

    def row_tap(t, k, count):
        at = slice((6 - k) * PITCH, (6 - k) * PITCH + count)
        return rows_hi[t, at], rows_lo[t, at]

    def padded(value):
        return jnp.concatenate(
            [value, jnp.zeros((height, PITCH - width, chans), value.dtype)], axis=1
        ).reshape(rows, chans)

    def transpose_acts(which, t):
        value = padded(acts[which, t])
        value = jnp.concatenate([value, jnp.zeros((256 - rows, chans), F32)], axis=0)
        high, low = split(value.T)
        act_t[which, t, 0] = high
        act_t[which, t, 1] = low

    def project(lhs, w):
        for k in range(taps):
            at = pl.ds(k * chans, chans)
            high, low = lhs(k)
            part = (
                dot_nt(high, w_hi[w, at]) + dot_nt(high, w_lo[w, at]) + dot_nt(low, w_hi[w, at])
            )
            if k == 0:
                total[...] = part
            else:
                total[...] += part

    def correlate(w, t, rhs):
        which = w
        for k in range(taps):
            at = pl.ds(k * chans, chans)
            high, low = rhs(k)
            a_hi, a_lo = act_t[which, t, 0], act_t[which, t, 1]
            part = dot_nn(a_hi, high) + dot_nn(a_hi, low) + dot_nn(a_lo, high)
            if t == 0:
                grads[w, at] = part
            else:
                grads[w, at] += part

    def set_cols(t):
        pre = total[...] * padded(masks[t]).astype(F32)
        column = lax.broadcasted_iota(jnp.int32, (rows, chans), 0) % PITCH
        for k in range(taps):
            by = k - 3
            moved = pre if by == 0 else pltpu.roll(pre, by % rows, 0)
            inside = (column >= by) & (column < PITCH + by)
            high, low = split(jnp.where(inside, moved, 0.0))
            cols_hi[k, 0:rows] = high
            cols_lo[k, 0:rows] = low

    def col_tap(count):
        return lambda k: (cols_hi[k, 0:count], cols_lo[k, 0:count])

    def give_map(t):
        out_map[t] = total[...].reshape(height, PITCH, chans)[:, :width]
        copy = pltpu.make_async_copy(out_map.at[t], data_grad.at[0, t, 0], store_sem.at[t])
        copy.start()
        return copy

    def pair_copy(w, xr, rel):
        return pltpu.make_async_remote_copy(
            src_ref=grads.at[w, block(xr, rel, True)],
            dst_ref=pair_in.at[w, slot(xr, rel)],
            send_sem=reduce_send.at[w],
            recv_sem=reduce_pair.at[w, slot(xr, rel)],
            device_id=pair,
            device_id_type=MESH,
        )

    def ring_copy(w, way, xr, hop):
        rel = way * (half + 1 - hop)
        lane = 0 if way == 1 else 1
        return pltpu.make_async_remote_copy(
            src_ref=grads.at[w, block(xr, rel)],
            dst_ref=ring_in.at[w, lane, hop - 1, xr],
            send_sem=reduce_send.at[w],
            recv_sem=reduce_ring.at[w, lane, hop - 1, xr],
            device_id=ahead[way],
            device_id_type=MESH,
        )

    def cross_copy(w):
        return pltpu.make_async_remote_copy(
            src_ref=grads.at[w, block(1, 0)],
            dst_ref=cross_in.at[w],
            send_sem=reduce_send.at[w],
            recv_sem=reduce_cross.at[w],
            device_id=cross,
            device_id_type=MESH,
        )

    def pair_start(w):
        for dist in range(half, -1, -1):
            for rel in (dist,) if dist in (0, half) else (dist, -dist):
                for xr in (0, 1):
                    pair_copy(w, xr, rel).start()

    def came(way, xr, hop):
        return hop >= 1 and (hop > 1 or xr == (0 if way == 1 else 1))

    def ring_hop(w, hop):
        for xr in (0, 1):
            for way in (1, -1):
                if not came(way, xr, hop):
                    continue
                rel = way * (half + 1 - hop)
                pair_copy(w, xr, rel).wait_recv()
                here = block(xr, rel)
                value = grads[w, here] + pair_in[w, slot(xr, rel)]
                if came(way, xr, hop - 1):
                    ring_copy(w, way, xr, hop - 1).wait_recv()
                    value = value + ring_in[w, 0 if way == 1 else 1, hop - 2, xr]
                grads[w, here] = value
                ring_copy(w, way, xr, hop).start()

    def ring_end(w):
        for xr in (1, 0):
            pair_copy(w, xr, 0).wait_recv()
            here = block(xr, 0)
            value = grads[w, here] + pair_in[w, slot(xr, 0)]
            for way in (1, -1):
                ring_copy(w, way, xr, half).wait_recv()
                value = value + ring_in[w, 0 if way == 1 else 1, half - 1, xr]
            grads[w, here] = value
            if xr == 1:
                cross_copy(w).start()

    def give_grad(w):
        cross_copy(w).wait_recv()
        grad_out[w] = (grads[w, block(0, 0)] + cross_in[w]) * (1.0 / (2 * replicas))
        out = (second_grad, first_grad)[w].at[0]
        copy = pltpu.make_async_copy(grad_out.at[w], out, store_sem.at[2 + w])
        copy.start()
        return copy

    stores = []
    gather_start(0)
    gather_start(1)
    rows_hi[...] = jnp.zeros_like(rows_hi)
    rows_lo[...] = jnp.zeros_like(rows_lo)
    cols_hi[:, rows:256] = jnp.zeros((taps, 256 - rows, chans), BF16)
    cols_lo[:, rows:256] = jnp.zeros((taps, 256 - rows, chans), BF16)
    loads[0].wait()
    set_rows(0, padded(ups[0]))
    loads[2].wait()
    transpose_acts(0, 0)
    gather_hop(1)
    correlate(0, 0, lambda k: row_tap(0, k, 256))
    for hop in range(2, half):
        gather_hop(hop)
    loads[3].wait()
    transpose_acts(0, 1)
    loads[6].wait()
    transpose_acts(1, 0)
    loads[7].wait()
    transpose_acts(1, 1)
    gather_end(0)
    gather_end(1)
    gather_pair_wait(0)
    round_weights(0)
    project(lambda k: row_tap(0, k, rows), 0)
    loads[4].wait()
    set_cols(0)
    gather_pair_wait(1)
    round_weights(1)
    project(col_tap(rows), 1)
    passed[...] = total[...]
    shift = pltpu.make_async_remote_copy(
        src_ref=passed,
        dst_ref=above,
        send_sem=shift_sem.at[0],
        recv_sem=shift_sem.at[1],
        device_id=prev_section,
        device_id_type=MESH,
    )
    shift.start()
    stores.append(give_map(0))
    correlate(1, 0, col_tap(256))
    loads[1].wait()
    loads[5].wait()
    shift.wait_recv()
    is_last = jnp.full((rows, chans), sec, jnp.int32) == sections - 1
    set_rows(1, jnp.where(is_last, padded(ups[1]), above[...]))
    correlate(0, 1, lambda k: row_tap(1, k, 256))
    pair_start(0)
    project(lambda k: row_tap(1, k, rows), 0)
    ring_hop(0, 1)
    set_cols(1)
    correlate(1, 1, col_tap(256))
    pair_start(1)
    ring_hop(0, 2)
    ring_hop(1, 1)
    for hop in range(3, half + 1):
        ring_hop(0, hop)
        ring_hop(1, hop - 1)
    project(col_tap(rows), 1)
    stores.append(give_map(1))
    ring_hop(1, half)
    ring_end(0)
    ring_end(1)
    stores.append(give_grad(0))
    stores.append(give_grad(1))

    shift.wait_send()
    sent = pl.ds(0, (4 * ny - 1) * shard)
    for w in range(2):
        for buffer, sem in ((weights, gather_send), (grads, reduce_send)):
            pltpu.make_async_remote_copy(
                src_ref=buffer.at[w, sent],
                dst_ref=buffer.at[w, sent],
                send_sem=sem.at[w],
                recv_sem=sem.at[w],
                device_id=pair,
                device_id_type=MESH,
            ).wait_send()
    for copy in stores:
        copy.wait()


def local(sections, replicas, *args):
    act_in, w_first = args[0], args[5]
    height, width, chans = act_in.shape[3:]
    shard = w_first.shape[1]
    all_rows = shard * replicas
    ny = replicas // 4
    rows = height * PITCH
    dma = pltpu.SemaphoreType.DMA
    anywhere = pl.BlockSpec(memory_space=pl.ANY)
    scratch = [
        pltpu.VMEM((2, 2, height, width, chans), F32),
        pltpu.VMEM((2, height, width, chans), jnp.int32),
        pltpu.VMEM((2, height, width, chans), F32),
        pltpu.VMEM((2, 2, 2, chans, 256), BF16),
        pltpu.VMEM((2, 6 * PITCH + 256, chans), BF16),
        pltpu.VMEM((2, 6 * PITCH + 256, chans), BF16),
        pltpu.VMEM((7, 256, chans), BF16),
        pltpu.VMEM((7, 256, chans), BF16),
        pltpu.VMEM((2, all_rows, chans), F32),
        pltpu.VMEM((2, all_rows, chans), BF16),
        pltpu.VMEM((2, all_rows, chans), BF16),
        pltpu.VMEM((rows, chans), F32),
        pltpu.VMEM((rows, chans), F32),
        pltpu.VMEM((rows, chans), F32),
        pltpu.VMEM((2, height, width, chans), F32),
        pltpu.VMEM((2, all_rows, chans), F32),
        pltpu.VMEM((2, 2 * ny, shard, chans), F32),
        pltpu.VMEM((2, 2, ny // 2, 2, shard, chans), F32),
        pltpu.VMEM((2, shard, chans), F32),
        pltpu.VMEM((2, shard, chans), F32),
        dma((8,)),
        dma((2,)),
        dma((2,)),
        dma((2, 2 * ny)),
        dma((2, 2 * ny)),
        dma((2,)),
        dma((2,)),
        dma((2, 2 * ny)),
        dma((2, 2, ny // 2, 2)),
        dma((2,)),
        dma((4,)),
    ]
    return pl.pallas_call(
        functools.partial(kernel, sections, replicas),
        out_shape=(
            jax.ShapeDtypeStruct(act_in.shape, F32),
            jax.ShapeDtypeStruct(w_first.shape, F32),
            jax.ShapeDtypeStruct(w_first.shape, F32),
        ),
        in_specs=[anywhere] * 7,
        out_specs=(anywhere,) * 3,
        scratch_shapes=scratch,
        compiler_params=pltpu.CompilerParams(collective_id=0, has_side_effects=True),
    )(*args)


def solution(mesh):
    return jax.shard_map(
        functools.partial(local, mesh.shape["section"], mesh.shape["dp"]),
        mesh=mesh,
        in_specs=(
            P("section", None, "dp", None, None, None),
            P("section", None, "dp", None, None, None),
            P("section", None, "dp", None, None, None),
            P("section", "dp", None, None, None),
            P(None, "dp", None, None, None),
            P("section", "dp", None),
            P("section", "dp", None),
        ),
        out_specs=(
            P("section", None, "dp", None, None, None),
            P("section", "dp", None),
            P("section", "dp", None),
        ),
        check_vma=False,
    )
```

time: 364 us -> 86.5 us (0.24)
  the two profiles are of different devices: /device:TPU:16 before, /device:TPU:128 now
where the time goes in v1:
time: 86.5 us; the launch traced here: 86.2 us
  Pallas kernels  76.1 us (88%)
  local copies, waits for them, and re-layouts  9.46 us (11%)
    pallas_call x1, Pallas kernels, local(): pl.pallas_call(functools.partial(kernel, sections, replicas), out_shape=(...  76.1 us
    unnamed x19, local copies, waits for them, and re-layouts  7.17 us
    pallas_call x1, local copies, waits for them, and re-layouts, local(): pl.pallas_call(functools.partial(kernel, sections, replicas), out_shape=(...  2.29 us

profile of v1, /device:TPU:128, one launch (start us, length us, event | category | flops | bytes accessed | tf_op | source)
XLA Modules:
  0.0 86.2 jit_solution(9726844810201887219)
XLA Ops:
  0.6 0.0 copy-start.3
  0.6 0.0 copy-start
  0.7 1.7 %copy.13.arriving = f32[1,1,15,15,256]{4,3,2,1,0:T(8,128)} copy(f32[1,1,15,15,256]{4,1,3,2,0:T(1,128)} %param.10) | data formatting | bytes 460800 | tf_op args[3]
  2.4 0.0 copy-done.3
  2.4 0.7 copy.14.loss_grad
  3.1 0.0 copy-done
  3.1 0.0 copy-start.1
  3.1 0.8 copy.10.act_in
  4.0 0.4 copy-done.1
  4.3 0.0 copy-start.2
  4.3 0.8 copy.11.act_mid
  5.2 0.4 copy-done.2
  5.5 0.9 copy.12.relu_mask
  6.4 76.1 %shard_map.94 = (f32[1,2,1,15,15,256]{5,4,3,2,1,0:T(8,128)}, f32[1,56,256]{2,1,0:T(8,128)}, f32[1,56,256]{2,1,0:T(8,128)}) custom-call(f32[1,2,1,15,15,256]{5,4,3,2,1,0:T(8,128)} %copy.10.act_in, f32[1,2,1,15,15,256]{5,4,3,2,1,0:T(8,128)} %copy.11.act_mid, s32[1,2,1,15,15,256]{5,4,3,2,1,0:T(8,128)} %copy.12.relu_mask, f32[1,1,15,15,256]{4,3,2,1,0:T(8,128)} %copy.13.arriving, ...), custom_call_target="tpu_custom_call" | custom-call | tf_op jit(solution)/shard_map/pallas_call | solution.py:451
  82.4 0.0 copy-start.5
  82.5 2.3 %copy.15 = f32[1,2,1,15,15,256]{5,2,4,3,1,0:T(1,128)} copy(f32[1,2,1,15,15,256]{5,4,3,2,1,0:T(8,128)} %get-tuple-element.3) | data formatting | bytes 921600 | tf_op jit(solution)/shard_map/pallas_call | solution.py:451
  84.7 0.0 copy-done.5
  84.7 0.0 copy-start.4
  84.7 0.6 copy.18
  85.4 0.2 copy-done.4
  85.6 0.6 copy.19
Async XLA Ops:
  0.6 1.7 %copy-start.3 = (f32[1,1,15,15,256]{4,1,3,2,0:T(1,128)S(1)}, f32[1,1,15,15,256]{4,1,3,2,0:T(1,128)}, u32[]{:S(2)}) copy-start(f32[1,1,15,15,256]{4,1,3,2,0:T(1,128)} %param.11) | copy-start | bytes 691204
  0.6 2.5 %copy-start = (f32[1,2,1,15,15,256]{5,2,4,3,1,0:T(1,128)S(1)}, f32[1,2,1,15,15,256]{5,2,4,3,1,0:T(1,128)}, u32[]{:S(2)}) copy-start(f32[1,2,1,15,15,256]{5,2,4,3,1,0:T(1,128)} %param.7) | copy-start | bytes 1382404
  3.1 1.2 %copy-start.1 = (f32[1,2,1,15,15,256]{5,2,4,3,1,0:T(1,128)S(1)}, f32[1,2,1,15,15,256]{5,2,4,3,1,0:T(1,128)}, u32[]{:S(2)}) copy-start(f32[1,2,1,15,15,256]{5,2,4,3,1,0:T(1,128)} %param.8) | copy-start | bytes 1382404
  4.3 1.2 %copy-start.2 = (s32[1,2,1,15,15,256]{5,2,4,3,1,0:T(1,128)S(1)}, s32[1,2,1,15,15,256]{5,2,4,3,1,0:T(1,128)}, u32[]{:S(2)}) copy-start(s32[1,2,1,15,15,256]{5,2,4,3,1,0:T(1,128)} %param.9) | copy-start | bytes 1382404
  82.4 2.3 %copy-start.5 = (f32[1,56,256]{2,1,0:T(8,128)S(1)}, f32[1,56,256]{2,1,0:T(8,128)}, u32[]{:S(2)}) copy-start(f32[1,56,256]{2,1,0:T(8,128)} %get-tuple-element.10) | copy-start | bytes 172036
  84.7 0.8 copy-start.4

commit v2 on v1

v2 whole, which is shorter than its diff:
```python
import functools

import jax
import jax.numpy as jnp
from jax import lax
from jax.experimental import pallas as pl
from jax.experimental.pallas import tpu as pltpu
from jax.sharding import PartitionSpec as P

MESH = pl.DeviceIdType.MESH
F32, BF16 = jnp.float32, jnp.bfloat16
HEIGHT, WIDTH = 15, 15
GATHER_A = (0, 56)
REDUCE_A = (56, 0)
PITCH = 16


def split(value):
    high = value.astype(BF16)
    return high, (value - high.astype(F32)).astype(BF16)


def dot_nt(a, b):
    return lax.dot_general(a, b, (((1,), (1,)), ((), ())), preferred_element_type=F32)


def dot_nn(a, b):
    return lax.dot_general(a, b, (((1,), (0,)), ((), ())), preferred_element_type=F32)


def kernel(
    sections,
    replicas,
    act_in,
    act_mid,
    relu_mask,
    arriving,
    loss_grad,
    w_first,
    w_second,
    data_grad,
    first_grad,
    second_grad,
    raw_acts,
    raw_mask,
    raw_up,
    flat,
    act_t,
    rows_hi,
    rows_lo,
    cols_hi,
    cols_lo,
    weights,
    w_hi,
    w_lo,
    total,
    passed,
    above,
    grads,
    pair_in,
    ring_in,
    cross_b_in,
    cross_a_in,
    load_sem,
    own_sem,
    gather_send,
    gather_ring,
    gather_cross,
    gather_pair,
    shift_sem,
    reduce_send,
    reduce_pair,
    reduce_ring,
    reduce_cross_b,
    reduce_cross_a,
):
    ny = replicas // 4
    half = ny // 2
    shard, chans = w_first.shape[1:]
    size = HEIGHT * WIDTH
    rows = HEIGHT * PITCH
    taps = 7
    sec = lax.axis_index("section")
    dp = lax.axis_index("dp")
    x, y, c = dp // (2 * ny), (dp // 2) % ny, dp % 2

    def device(xr, rel, other):
        xx = 1 - x if xr else x
        cc = 1 - c if other else c
        return xx * (2 * ny) + lax.rem(y + rel + ny, ny) * 2 + cc

    def block(xr, rel, other=False, low=0, count=shard):
        return pl.ds(pl.multiple_of(device(xr, rel, other) * shard + low, 8), count)

    def slot(xr, rel):
        return xr * ny + rel % ny

    pair = {"dp": device(0, 0, True)}
    cross = {"dp": device(1, 0, False)}
    ahead = {1: {"dp": device(0, 1, False)}, -1: {"dp": device(0, -1, False)}}
    prev_section = {"section": lax.rem(sec + sections - 1, sections)}
    next_section = {"section": lax.rem(sec + 1, sections)}

    barrier = pltpu.get_barrier_semaphore()
    friends = (pair, cross, ahead[1], ahead[-1], prev_section, next_section)
    for friend in friends:
        pl.semaphore_signal(barrier, inc=1, device_id=friend, device_id_type=MESH)

    sources = (arriving, act_mid, act_in, relu_mask, loss_grad)
    targets = (raw_up.at[0], raw_acts.at[0], raw_acts.at[1], raw_mask, raw_up.at[1])
    loads = [
        pltpu.make_async_copy(s, d, load_sem.at[i])
        for i, (s, d) in enumerate(zip(sources, targets))
    ]
    for copy in loads:
        copy.start()
    shards = (w_second.at[0], w_first.at[0])
    own = [
        pltpu.make_async_copy(shards[w], weights.at[w, block(0, 0)], own_sem.at[w])
        for w in range(2)
    ]
    for copy in own:
        copy.start()

    def copy_to(src, dst, send_sem, recv_sem, to):
        return pltpu.make_async_remote_copy(
            src_ref=src,
            dst_ref=dst,
            send_sem=send_sem,
            recv_sem=recv_sem,
            device_id=to,
            device_id_type=MESH,
        )

    def allowed(w, way, xr, hop, last):
        return hop != last or (xr == 0) == ((way == 1) == (w == 0))

    def span(w, xr, first=GATHER_A):
        return (0, first[w]) if xr else (0, shard)

    def rest(w, first):
        return first[w], shard - first[w]

    def gather_ring_copy(w, way, xr, hop):
        at = block(xr, -way * hop, False, *span(w, xr))
        here = weights.at[w, at]
        sem = gather_ring.at[w, slot(xr, -way * hop)]
        return copy_to(here, here, gather_send.at[w], sem, ahead[way])

    def gather_on(w, way, xr, hop, src=None):
        if span(w, xr)[1] == 0:
            return
        here = weights.at[w, block(xr, -way * (hop - 1), False, *span(w, xr))]
        sem = gather_ring.at[w, slot(xr, -way * hop)]
        copy_to(here if src is None else src, here, gather_send.at[w], sem, ahead[way]).start()

    def gather_cross_copy(w, rel, sending, src=None):
        low, count = (0, shard) if rel == 0 else rest(w, GATHER_A)
        here = weights.at[w, block(0 if sending else 1, rel, False, low, count)]
        sem = gather_cross.at[w, rel % ny]
        return copy_to(here if src is None else src, here, gather_send.at[w], sem, cross)

    def gather_pair_copy(w, xr, rel, piece, sending, src=None):
        low, count = rest(w, GATHER_A) if piece else (0, shard)
        if piece == 0 and xr == 1 and rel % ny:
            count = GATHER_A[w]
        here = weights.at[w, block(xr, rel, not sending, low, count)]
        sem = gather_pair.at[w, slot(xr, rel), piece]
        return copy_to(here if src is None else src, here, gather_send.at[w], sem, pair)

    def gather_start(w):
        src = shards[w]
        gather_on(w, 1, 0, 1, src)
        gather_on(w, -1, 0, 1, src)
        gather_cross_copy(w, 0, True, src).start()
        gather_pair_copy(w, 0, 0, 0, True, src).start()

    def ring_arrival(w, way, xr, hop):
        if span(w, xr)[1] == 0:
            return
        gather_ring_copy(w, way, xr, hop).wait_recv()
        if hop < half and allowed(w, way, xr, hop + 1, half):
            gather_on(w, way, xr, hop + 1)
        if xr == 0 and GATHER_A[w] < shard:
            gather_cross_copy(w, -way * hop, True).start()
        gather_pair_copy(w, xr, -way * hop, 0, True).start()

    def cross_arrival(w, rel):
        if rel and GATHER_A[w] == shard:
            return
        gather_cross_copy(w, rel, False).wait_recv()
        if rel == 0:
            gather_on(w, 1, 1, 1)
            gather_on(w, -1, 1, 1)
            gather_pair_copy(w, 1, 0, 0, True).start()
        else:
            gather_pair_copy(w, 1, rel, 1, True).start()

    def gather_hop(w, xr, hop):
        for way in (1, -1):
            if allowed(w, way, xr, hop, half):
                ring_arrival(w, way, xr, hop)

    def gather_cross_hop(w, dist):
        for rel in (dist,) if dist in (0, half) else (dist, -dist):
            cross_arrival(w, rel)

    def gather_pair_wait(w):
        own[w].wait()
        for rel in range(ny):
            for xr in (0, 1):
                if xr == 0 or rel == 0 or GATHER_A[w]:
                    gather_pair_copy(w, xr, rel, 0, False).wait_recv()
            if rel and GATHER_A[w] < shard:
                gather_pair_copy(w, 1, rel, 1, False).wait_recv()

    def round_weights(w):
        high, low = split(weights[w])
        w_hi[w] = high
        w_lo[w] = low

    top = 3 * PITCH

    def flatten(raw, start, to):
        zero = jnp.zeros((PITCH - WIDTH, chans), F32)
        for h in range(HEIGHT):
            line = raw[pl.ds(start + h * WIDTH, WIDTH), 0, :].astype(F32)
            flat[to, h * PITCH : (h + 1) * PITCH] = jnp.concatenate([line, zero], axis=0)

    def set_rows(t, value):
        high, low = split(value)
        rows_hi[t, top : top + rows] = high
        rows_lo[t, top : top + rows] = low

    def row_tap(t, k, count):
        at = slice((6 - k) * PITCH, (6 - k) * PITCH + count)
        return rows_hi[t, at], rows_lo[t, at]

    def transpose_acts(which, t):
        flatten(raw_acts.at[which], t * size, 0)
        high, low = split(flat[0].T)
        act_t[which, t, 0] = high
        act_t[which, t, 1] = low

    def project(lhs, w, first=0, last=7):
        for k in range(first, last):
            at = pl.ds(k * chans, chans)
            high, low = lhs(k)
            part = (
                dot_nt(high, w_hi[w, at]) + dot_nt(high, w_lo[w, at]) + dot_nt(low, w_hi[w, at])
            )
            if k == 0:
                total[...] = part
            else:
                total[...] += part

    def correlate(w, t, rhs):
        for k in range(taps):
            at = pl.ds(k * chans, chans)
            high, low = rhs(k)
            a_hi, a_lo = act_t[w, t, 0], act_t[w, t, 1]
            part = dot_nn(a_hi, high) + dot_nn(a_hi, low) + dot_nn(a_lo, high)
            if t == 0:
                grads[w, at] = part
            else:
                grads[w, at] += part

    def set_cols(t):
        pre = total[...] * flat[1 + t, 0:rows]
        column = lax.broadcasted_iota(jnp.int32, (rows, chans), 0) % PITCH
        for k in range(taps):
            by = k - 3
            moved = pre if by == 0 else pltpu.roll(pre, by % rows, 0)
            inside = (column >= by) & (column < PITCH + by)
            high, low = split(jnp.where(inside, moved, 0.0))
            cols_hi[k, 0:rows] = high
            cols_lo[k, 0:rows] = low

    def col_tap(count):
        return lambda k: (cols_hi[k, 0:count], cols_lo[k, 0:count])

    def give_map(t):
        for h in range(HEIGHT):
            line = total[h * PITCH : (h + 1) * PITCH]
            data_grad[pl.ds(t * size + h * WIDTH, WIDTH), 0, :] = line[0:WIDTH]

    def pair_copy(w, xr, rel):
        return copy_to(
            grads.at[w, block(xr, rel, True)],
            pair_in.at[w, slot(xr, rel)],
            reduce_send.at[w],
            reduce_pair.at[w, slot(xr, rel)],
            pair,
        )

    def ring_copy(w, way, xr, hop):
        rel = way * (half + 1 - hop)
        lane = 0 if way == 1 else 1
        low, count = span(w, xr, REDUCE_A)
        return copy_to(
            grads.at[w, block(xr, rel, False, low, count)],
            ring_in.at[w, lane, hop - 1, xr, pl.ds(low, count)],
            reduce_send.at[w],
            reduce_ring.at[w, lane, hop - 1, xr],
            ahead[way],
        )

    def cross_b_copy(w, rel):
        return copy_to(
            grads.at[w, block(1, rel, False, *rest(w, REDUCE_A))],
            cross_b_in.at[w, rel % ny, pl.ds(*rest(w, REDUCE_A))],
            reduce_send.at[w],
            reduce_cross_b.at[w, rel % ny],
            cross,
        )

    def cross_a_copy(w):
        return copy_to(
            grads.at[w, block(1, 0, False, 0, REDUCE_A[w])],
            cross_a_in.at[w, pl.ds(0, REDUCE_A[w])],
            reduce_send.at[w],
            reduce_cross_a.at[w],
            cross,
        )

    outward = [half]
    for dist in range(half - 1, 0, -1):
        outward += [dist, -dist]
    outward.append(0)

    def pair_start(w):
        for rel in outward:
            for xr in (1, 0):
                pair_copy(w, xr, rel).start()

    def cross_hop(w):
        for rel in outward:
            pair_copy(w, 1, rel).wait_recv()
            here = block(1, rel)
            grads[w, here] += pair_in[w, slot(1, rel)]
            if REDUCE_A[w] < shard:
                cross_b_copy(w, rel).start()

    def came(w, way, xr, hop):
        return hop >= 1 and allowed(w, way, xr, hop, 1) and span(w, xr, REDUCE_A)[1] > 0

    def lane_of(way):
        return 0 if way == 1 else 1

    def own_column(w, rel):
        pair_copy(w, 0, rel).wait_recv()
        here = block(0, rel)
        grads[w, here] += pair_in[w, slot(0, rel)]
        if REDUCE_A[w] < shard:
            cross_b_copy(w, rel).wait_recv()
            low, count = rest(w, REDUCE_A)
            here = block(0, rel, False, low, count)
            grads[w, here] += cross_b_in[w, rel % ny, low : low + count]

    def ring_hop(w, hop, columns=(1, 0)):
        for xr in columns:
            for way in (1, -1):
                if not came(w, way, xr, hop):
                    continue
                rel = way * (half + 1 - hop)
                if xr == 0:
                    own_column(w, rel)
                if came(w, way, xr, hop - 1):
                    ring_copy(w, way, xr, hop - 1).wait_recv()
                    low, count = span(w, xr, REDUCE_A)
                    here = block(xr, rel, False, low, count)
                    grads[w, here] += ring_in[w, lane_of(way), hop - 2, xr, low : low + count]
                ring_copy(w, way, xr, hop).start()

    def ring_end(w):
        for xr in (1, 0):
            low, count = span(w, xr, REDUCE_A)
            if count == 0:
                continue
            here = block(xr, 0, False, low, count)
            if xr == 0:
                own_column(w, 0)
            for way in (1, -1):
                ring_copy(w, way, xr, half).wait_recv()
            grads[w, here] += (
                ring_in[w, 0, half - 1, xr, low : low + count]
                + ring_in[w, 1, half - 1, xr, low : low + count]
            )
            if xr == 1:
                cross_a_copy(w).start()

    def give_grad(w):
        scale = 1.0 / (2 * replicas)
        low, count = rest(w, REDUCE_A)
        grad_out = (second_grad, first_grad)[w]
        if low:
            cross_a_copy(w).wait_recv()
            first = grads[w, block(0, 0, False, 0, low)] + cross_a_in[w, 0:low]
            grad_out[0, 0:low] = first * scale
        if count:
            grad_out[0, low:shard] = grads[w, block(0, 0, False, low, count)] * scale

    rows_hi[...] = jnp.zeros_like(rows_hi)
    rows_lo[...] = jnp.zeros_like(rows_lo)
    cols_hi[:, rows:256] = jnp.zeros((taps, 256 - rows, chans), BF16)
    cols_lo[:, rows:256] = jnp.zeros((taps, 256 - rows, chans), BF16)
    flat[0, rows:256] = jnp.zeros((256 - rows, chans), F32)
    pl.semaphore_wait(barrier, len(friends))
    gather_start(0)
    loads[0].wait()
    flatten(raw_up.at[0], 0, 1)
    set_rows(0, flat[1, 0:rows])
    loads[1].wait()
    transpose_acts(0, 0)
    transpose_acts(0, 1)
    loads[2].wait()
    transpose_acts(1, 0)
    transpose_acts(1, 1)
    gather_start(1)
    loads[3].wait()
    for t in range(2):
        flatten(raw_mask, t * size, 1 + t)
    loads[4].wait()
    flatten(raw_up.at[1], 0, 3)
    gather_hop(0, 0, 1)
    gather_hop(1, 0, 1)
    gather_cross_hop(0, 0)
    gather_cross_hop(1, 0)
    for hop in range(2, half + 1):
        gather_hop(0, 0, hop)
        gather_hop(0, 1, hop - 1)
        if hop > 2:
            gather_hop(1, 1, hop - 2)
        else:
            correlate(0, 0, lambda k: row_tap(0, k, 256))
        gather_hop(1, 0, hop)
        if hop > 2:
            gather_cross_hop(0, hop - 2)
    gather_hop(0, 1, half)
    gather_hop(1, 1, half - 1)
    gather_cross_hop(0, half - 1)
    gather_cross_hop(0, half)
    for dist in range(1, half - 1):
        gather_cross_hop(1, dist)
    gather_hop(1, 1, half)
    gather_pair_wait(0)
    round_weights(0)
    project(lambda k: row_tap(0, k, rows), 0, 0, 3)
    gather_cross_hop(1, half - 1)
    project(lambda k: row_tap(0, k, rows), 0, 3, 7)
    gather_cross_hop(1, half)
    set_cols(0)
    gather_pair_wait(1)
    round_weights(1)
    project(col_tap(rows), 1)
    passed[...] = total[...]
    shift = copy_to(passed, above, shift_sem.at[0], shift_sem.at[1], prev_section)
    shift.start()
    give_map(0)
    correlate(1, 0, col_tap(256))
    shift.wait_recv()
    is_last = jnp.full((rows, chans), sec, jnp.int32) == sections - 1
    set_rows(1, jnp.where(is_last, flat[3, 0:rows], above[...]))
    correlate(0, 1, lambda k: row_tap(1, k, 256))
    pair_start(0)
    project(lambda k: row_tap(1, k, rows), 0)
    cross_hop(0)
    ring_hop(0, 1, (1,))
    set_cols(1)
    correlate(1, 1, col_tap(256))
    pair_start(1)
    ring_hop(0, 1, (0,))
    cross_hop(1)
    ring_hop(0, 2)
    ring_hop(1, 1)
    if half > 2:
        ring_hop(0, 3)
    project(col_tap(rows), 1, 0, 3)
    ring_hop(1, 2)
    if half > 2:
        ring_hop(0, 4)
    project(col_tap(rows), 1, 3, 7)
    give_map(1)
    if half > 2:
        ring_hop(1, 3)
    ring_end(0)
    if half > 2:
        ring_hop(1, 4)
    give_grad(0)
    ring_end(1)
    give_grad(1)

    shift.wait_send()
    sent = pl.ds(0, (4 * ny - 1) * shard)
    for w in range(2):
        for buffer, sem in ((weights, gather_send), (grads, reduce_send)):
            there = buffer.at[w, sent]
            copy_to(there, there, sem.at[w], sem.at[w], pair).wait_send()


def local(sections, replicas, *args):
    act_in, w_first = args[0], args[5]
    chans = act_in.shape[-1]
    shard = w_first.shape[1]
    all_rows = shard * replicas
    ny = replicas // 4
    rows, size = HEIGHT * PITCH, HEIGHT * WIDTH
    dma = pltpu.SemaphoreType.DMA
    anywhere = pl.BlockSpec(memory_space=pl.ANY)
    scratch = [
        pltpu.VMEM((2, 2 * size, 1, chans), F32),
        pltpu.VMEM((2 * size, 1, chans), jnp.int32),
        pltpu.VMEM((2, size, 1, chans), F32),
        pltpu.VMEM((4, 256, chans), F32),
        pltpu.VMEM((2, 2, 2, chans, 256), BF16),
        pltpu.VMEM((2, 6 * PITCH + 256, chans), BF16),
        pltpu.VMEM((2, 6 * PITCH + 256, chans), BF16),
        pltpu.VMEM((7, 256, chans), BF16),
        pltpu.VMEM((7, 256, chans), BF16),
        pltpu.VMEM((2, all_rows, chans), F32),
        pltpu.VMEM((2, all_rows, chans), BF16),
        pltpu.VMEM((2, all_rows, chans), BF16),
        pltpu.VMEM((rows, chans), F32),
        pltpu.VMEM((rows, chans), F32),
        pltpu.VMEM((rows, chans), F32),
        pltpu.VMEM((2, all_rows, chans), F32),
        pltpu.VMEM((2, 2 * ny, shard, chans), F32),
        pltpu.VMEM((2, 2, ny // 2, 2, shard, chans), F32),
        pltpu.VMEM((2, ny, shard, chans), F32),
        pltpu.VMEM((2, shard, chans), F32),
        dma((5,)),
        dma((2,)),
        dma((2,)),
        dma((2, 2 * ny)),
        dma((2, ny)),
        dma((2, 2 * ny, 2)),
        dma((2,)),
        dma((2,)),
        dma((2, 2 * ny)),
        dma((2, 2, ny // 2, 2)),
        dma((2, ny)),
        dma((2,)),
    ]
    maps, first, second = pl.pallas_call(
        functools.partial(kernel, sections, replicas),
        out_shape=(
            pltpu.VMEM((2 * size, 1, chans), F32),
            pltpu.VMEM(w_first.shape, F32),
            pltpu.VMEM(w_first.shape, F32),
        ),
        in_specs=[anywhere] * 7,
        out_specs=(pl.BlockSpec(memory_space=pltpu.VMEM),) * 3,
        scratch_shapes=scratch,
        compiler_params=pltpu.CompilerParams(collective_id=0, has_side_effects=True),
    )(*(a.reshape(-1, 1, chans) for a in args[:5]), *args[5:])
    return maps.reshape(act_in.shape), first, second


def solution(mesh):
    return jax.shard_map(
        functools.partial(local, mesh.shape["section"], mesh.shape["dp"]),
        mesh=mesh,
        in_specs=(
            P("section", None, "dp", None, None, None),
            P("section", None, "dp", None, None, None),
            P("section", None, "dp", None, None, None),
            P("section", "dp", None, None, None),
            P(None, "dp", None, None, None),
            P("section", "dp", None),
            P("section", "dp", None),
        ),
        out_specs=(
            P("section", None, "dp", None, None, None),
            P("section", "dp", None),
            P("section", "dp", None),
        ),
        check_vma=False,
    )
```

time: 86.5 us -> 71.5 us (0.83)
  the two profiles are of different devices: /device:TPU:128 before, /device:TPU:130 now
where the time goes in v2:
time: 71.5 us; the launch traced here: 71.3 us
  Pallas kernels  68.7 us (96%)
  local copies, waits for them, and re-layouts  2.02 us (3%)
    pallas_call x1, Pallas kernels, local(): pl.pallas_call(functools.partial(kernel, sections, replicas), out_shape=(...  68.7 us
    unnamed x3, local copies, waits for them, and re-layouts  2.02 us

profile of v2, /device:TPU:130, one launch (start us, length us, event | category | flops | bytes accessed | tf_op | source)
XLA Modules:
  0.0 71.3 jit_solution(18273994045132316279)
XLA Ops:
  0.6 68.7 %shard_map.94 = (f32[450,1,256]{2,1,0:T(1,128)S(1)}, f32[1,56,256]{2,1,0:T(8,128)S(1)}, f32[1,56,256]{2,1,0:T(8,128)S(1)}) custom-call(f32[450,1,256]{2,1,0:T(1,128)} %bitcast.9, f32[450,1,256]{2,1,0:T(1,128)} %bitcast.10, s32[450,1,256]{2,1,0:T(1,128)} %bitcast.11, f32[225,1,256]{2,1,0:T(1,128)} %bitcast.12, f32[225,1,256]{2,1,0:T(1,128)} %bitcast.13, ...), custom_call_target="tpu_custom_call" | custom-call | tf_op jit(solution)/shard_map/pallas_call | solution.py:544
  69.3 0.8 %copy.14 = f32[1,2,1,15,15,256]{5,2,4,3,1,0:T(1,128)} copy(f32[1,2,1,15,15,256]{5,2,4,3,1,0:T(1,128)S(1)} %bitcast.8) | data formatting | bytes 921600
  70.1 0.6 copy.15
  70.7 0.6 copy.16

commit v3 on v2

--- a/solution.py
+++ b/solution.py
@@ -12,6 +12,7 @@
 HEIGHT, WIDTH = 15, 15
 GATHER_A = (0, 56)
 REDUCE_A = (56, 0)
+PIECES = ((0, 56),), ((0, 32), (32, 24))
 PITCH = 16
 
 
@@ -39,8 +40,7 @@
     w_first,
     w_second,
     data_grad,
-    first_grad,
-    second_grad,
+    both_grads,
     raw_acts,
     raw_mask,
     raw_up,
@@ -293,24 +293,37 @@
             pair,
         )
 
-    def ring_copy(w, way, xr, hop):
+    def piece(w, xr, part, first=REDUCE_A):
+        low, count = PIECES[w][part]
+        return low, min(low + count, span(w, xr, first)[1]) - low
+
+    def parts(w, xr):
+        return [p for p in range(len(PIECES[w])) if piece(w, xr, p)[1] > 0]
+
+    def ring_copy(w, way, xr, hop, part):
         rel = way * (half + 1 - hop)
         lane = 0 if way == 1 else 1
-        low, count = span(w, xr, REDUCE_A)
+        low, count = piece(w, xr, part)
         return copy_to(
             grads.at[w, block(xr, rel, False, low, count)],
             ring_in.at[w, lane, hop - 1, xr, pl.ds(low, count)],
             reduce_send.at[w],
-            reduce_ring.at[w, lane, hop - 1, xr],
+            reduce_ring.at[w, lane, hop - 1, xr, part],
             ahead[way],
         )
 
-    def cross_b_copy(w, rel):
+    def b_piece(w, part):
+        low, count = PIECES[w][part]
+        start = max(low, REDUCE_A[w])
+        return start, low + count - start
+
+    def cross_b_copy(w, rel, part):
+        low, count = b_piece(w, part)
         return copy_to(
-            grads.at[w, block(1, rel, False, *rest(w, REDUCE_A))],
-            cross_b_in.at[w, rel % ny, pl.ds(*rest(w, REDUCE_A))],
+            grads.at[w, block(1, rel, False, low, count)],
+            cross_b_in.at[w, rel % ny, pl.ds(low, count)],
             reduce_send.at[w],
-            reduce_cross_b.at[w, rel % ny],
+            reduce_cross_b.at[w, rel % ny, part],
             cross,
         )
 
@@ -333,13 +346,14 @@
             for xr in (1, 0):
                 pair_copy(w, xr, rel).start()
 
-    def cross_hop(w):
-        for rel in outward:
+    def cross_hop(w, rels=outward):
+        for rel in rels:
             pair_copy(w, 1, rel).wait_recv()
             here = block(1, rel)
             grads[w, here] += pair_in[w, slot(1, rel)]
-            if REDUCE_A[w] < shard:
-                cross_b_copy(w, rel).start()
+            for part in range(len(PIECES[w])):
+                if b_piece(w, part)[1] > 0:
+                    cross_b_copy(w, rel, part).start()
 
     def came(w, way, xr, hop):
         return hop >= 1 and allowed(w, way, xr, hop, 1) and span(w, xr, REDUCE_A)[1] > 0
@@ -347,66 +361,66 @@
     def lane_of(way):
         return 0 if way == 1 else 1
 
-    def own_column(w, rel):
-        pair_copy(w, 0, rel).wait_recv()
-        here = block(0, rel)
-        grads[w, here] += pair_in[w, slot(0, rel)]
-        if REDUCE_A[w] < shard:
-            cross_b_copy(w, rel).wait_recv()
-            low, count = rest(w, REDUCE_A)
+    def own_column(w, rel, part):
+        if part == 0:
+            pair_copy(w, 0, rel).wait_recv()
+            here = block(0, rel)
+            grads[w, here] += pair_in[w, slot(0, rel)]
+        low, count = b_piece(w, part)
+        if count > 0:
+            cross_b_copy(w, rel, part).wait_recv()
             here = block(0, rel, False, low, count)
             grads[w, here] += cross_b_in[w, rel % ny, low : low + count]
 
-    def ring_hop(w, hop, columns=(1, 0)):
+    def ring_hop(w, hop):
+        for xr in (1, 0):
+            for part in parts(w, xr):
+                for way in (1, -1):
+                    if not came(w, way, xr, hop):
+                        continue
+                    rel = way * (half + 1 - hop)
+                    if xr == 0:
+                        own_column(w, rel, part)
+                    if came(w, way, xr, hop - 1):
+                        ring_copy(w, way, xr, hop - 1, part).wait_recv()
+                        low, count = piece(w, xr, part)
+                        here = block(xr, rel, False, low, count)
+                        lane = lane_of(way)
+                        grads[w, here] += ring_in[w, lane, hop - 2, xr, low : low + count]
+                    ring_copy(w, way, xr, hop, part).start()
+
+    def ring_end(w, columns=(1, 0)):
         for xr in columns:
-            for way in (1, -1):
-                if not came(w, way, xr, hop):
-                    continue
-                rel = way * (half + 1 - hop)
+            for part in parts(w, xr):
+                low, count = piece(w, xr, part)
+                here = block(xr, 0, False, low, count)
                 if xr == 0:
-                    own_column(w, rel)
-                if came(w, way, xr, hop - 1):
-                    ring_copy(w, way, xr, hop - 1).wait_recv()
-                    low, count = span(w, xr, REDUCE_A)
-                    here = block(xr, rel, False, low, count)
-                    grads[w, here] += ring_in[w, lane_of(way), hop - 2, xr, low : low + count]
-                ring_copy(w, way, xr, hop).start()
-
-    def ring_end(w):
-        for xr in (1, 0):
-            low, count = span(w, xr, REDUCE_A)
-            if count == 0:
-                continue
-            here = block(xr, 0, False, low, count)
-            if xr == 0:
-                own_column(w, 0)
-            for way in (1, -1):
-                ring_copy(w, way, xr, half).wait_recv()
-            grads[w, here] += (
-                ring_in[w, 0, half - 1, xr, low : low + count]
-                + ring_in[w, 1, half - 1, xr, low : low + count]
-            )
-            if xr == 1:
+                    own_column(w, 0, part)
+                for way in (1, -1):
+                    ring_copy(w, way, xr, half, part).wait_recv()
+                grads[w, here] += (
+                    ring_in[w, 0, half - 1, xr, low : low + count]
+                    + ring_in[w, 1, half - 1, xr, low : low + count]
+                )
+            if xr == 1 and REDUCE_A[w]:
                 cross_a_copy(w).start()
 
     def give_grad(w):
-        scale = 1.0 / (2 * replicas)
         low, count = rest(w, REDUCE_A)
-        grad_out = (second_grad, first_grad)[w]
         if low:
             cross_a_copy(w).wait_recv()
             first = grads[w, block(0, 0, False, 0, low)] + cross_a_in[w, 0:low]
-            grad_out[0, 0:low] = first * scale
+            both_grads[w, 0:low] = first
         if count:
-            grad_out[0, low:shard] = grads[w, block(0, 0, False, low, count)] * scale
-
+            both_grads[w, low:shard] = grads[w, block(0, 0, False, low, count)]
+
+    pl.semaphore_wait(barrier, len(friends))
+    gather_start(0)
     rows_hi[...] = jnp.zeros_like(rows_hi)
     rows_lo[...] = jnp.zeros_like(rows_lo)
     cols_hi[:, rows:256] = jnp.zeros((taps, 256 - rows, chans), BF16)
     cols_lo[:, rows:256] = jnp.zeros((taps, 256 - rows, chans), BF16)
     flat[0, rows:256] = jnp.zeros((256 - rows, chans), F32)
-    pl.semaphore_wait(barrier, len(friends))
-    gather_start(0)
     loads[0].wait()
     flatten(raw_up.at[0], 0, 1)
     set_rows(0, flat[1, 0:rows])
@@ -428,27 +442,19 @@
     gather_cross_hop(1, 0)
     for hop in range(2, half + 1):
         gather_hop(0, 0, hop)
+        gather_hop(1, 0, hop)
         gather_hop(0, 1, hop - 1)
-        if hop > 2:
-            gather_hop(1, 1, hop - 2)
-        else:
-            correlate(0, 0, lambda k: row_tap(0, k, 256))
-        gather_hop(1, 0, hop)
-        if hop > 2:
-            gather_cross_hop(0, hop - 2)
+        gather_hop(1, 1, hop - 1)
+        gather_cross_hop(0, hop - 1)
     gather_hop(0, 1, half)
-    gather_hop(1, 1, half - 1)
-    gather_cross_hop(0, half - 1)
     gather_cross_hop(0, half)
-    for dist in range(1, half - 1):
-        gather_cross_hop(1, dist)
-    gather_hop(1, 1, half)
     gather_pair_wait(0)
     round_weights(0)
-    project(lambda k: row_tap(0, k, rows), 0, 0, 3)
-    gather_cross_hop(1, half - 1)
-    project(lambda k: row_tap(0, k, rows), 0, 3, 7)
-    gather_cross_hop(1, half)
+    project(lambda k: row_tap(0, k, rows), 0, 0, 2)
+    gather_hop(1, 1, half)
+    for dist in range(1, half + 1):
+        gather_cross_hop(1, dist)
+    project(lambda k: row_tap(0, k, rows), 0, 2, 7)
     set_cols(0)
     gather_pair_wait(1)
     round_weights(1)
@@ -458,6 +464,7 @@
     shift.start()
     give_map(0)
     correlate(1, 0, col_tap(256))
+    correlate(0, 0, lambda k: row_tap(0, k, 256))
     shift.wait_recv()
     is_last = jnp.full((rows, chans), sec, jnp.int32) == sections - 1
     set_rows(1, jnp.where(is_last, flat[3, 0:rows], above[...]))
@@ -465,27 +472,28 @@
     pair_start(0)
     project(lambda k: row_tap(1, k, rows), 0)
     cross_hop(0)
-    ring_hop(0, 1, (1,))
+    ring_hop(0, 1)
     set_cols(1)
     correlate(1, 1, col_tap(256))
     pair_start(1)
-    ring_hop(0, 1, (0,))
-    cross_hop(1)
-    ring_hop(0, 2)
+    cross_hop(1, outward[:1])
+    if half > 2:
+        ring_hop(0, 2)
+    cross_hop(1, outward[1:])
     ring_hop(1, 1)
-    if half > 2:
-        ring_hop(0, 3)
-    project(col_tap(rows), 1, 0, 3)
-    ring_hop(1, 2)
-    if half > 2:
-        ring_hop(0, 4)
+    for hop in range(2, half):
+        ring_hop(0, hop + 1)
+        if hop == 2:
+            project(col_tap(rows), 1, 0, 3)
+        ring_hop(1, hop)
+    if half == 2:
+        project(col_tap(rows), 1, 0, 3)
+        ring_hop(0, 2)
     project(col_tap(rows), 1, 3, 7)
     give_map(1)
-    if half > 2:
-        ring_hop(1, 3)
-    ring_end(0)
-    if half > 2:
-        ring_hop(1, 4)
+    ring_end(0, (1,))
+    ring_hop(1, half)
+    ring_end(0, (0,))
     give_grad(0)
     ring_end(1)
     give_grad(1)
@@ -537,23 +545,23 @@
         dma((2,)),
         dma((2,)),
         dma((2, 2 * ny)),
-        dma((2, 2, ny // 2, 2)),
-        dma((2, ny)),
+        dma((2, 2, ny // 2, 2, 2)),
+        dma((2, ny, 2)),
         dma((2,)),
     ]
-    maps, first, second = pl.pallas_call(
+    maps, both = pl.pallas_call(
         functools.partial(kernel, sections, replicas),
         out_shape=(
             pltpu.VMEM((2 * size, 1, chans), F32),
-            pltpu.VMEM(w_first.shape, F32),
-            pltpu.VMEM(w_first.shape, F32),
+            pltpu.VMEM((2, shard, chans), F32),
         ),
         in_specs=[anywhere] * 7,
-        out_specs=(pl.BlockSpec(memory_space=pltpu.VMEM),) * 3,
+        out_specs=(pl.BlockSpec(memory_space=pltpu.VMEM),) * 2,
         scratch_shapes=scratch,
         compiler_params=pltpu.CompilerParams(collective_id=0, has_side_effects=True),
     )(*(a.reshape(-1, 1, chans) for a in args[:5]), *args[5:])
-    return maps.reshape(act_in.shape), first, second
+    both = both * (1.0 / (2 * replicas))
+    return maps.reshape(act_in.shape), both[1:], both[:1]
 
 
 def solution(mesh):

time: 71.5 us -> 69 us (0.965)
  the two profiles are of different devices: /device:TPU:130 before, /device:TPU:192 now
where the time goes in v3:
time: 69 us; the launch traced here: 68.8 us
  Pallas kernels  66.8 us (97%)
  local copies, waits for them, and re-layouts  1.42 us (2%)
    pallas_call x1, Pallas kernels, local(): pl.pallas_call(functools.partial(kernel, sections, replicas), out_shape=(...  66.8 us

profile of v3, /device:TPU:192, one launch (start us, length us, event | category | flops | bytes accessed | tf_op | source)
XLA Modules:
  0.0 68.8 jit_solution(13979314399312409913)
XLA Ops:
  0.6 66.8 %shard_map.94 = (f32[450,1,256]{2,1,0:T(1,128)S(1)}, f32[2,56,256]{2,1,0:T(8,128)S(1)}) custom-call(f32[450,1,256]{2,1,0:T(1,128)} %bitcast.9, f32[450,1,256]{2,1,0:T(1,128)} %bitcast.10, s32[450,1,256]{2,1,0:T(1,128)} %bitcast.11, f32[225,1,256]{2,1,0:T(1,128)} %bitcast.12, f32[225,1,256]{2,1,0:T(1,128)} %bitcast.13, f32[1,56,256]{2,1,0:T(8,128)} %w_first.1, ...), custom_call_target="tpu_custom_call" | custom-call | tf_op jit(solution)/shard_map/pallas_call | solution.py:552
  67.4 0.8 %copy.12 = f32[1,2,1,15,15,256]{5,2,4,3,1,0:T(1,128)} copy(f32[1,2,1,15,15,256]{5,2,4,3,1,0:T(1,128)S(1)} %bitcast.8) | data formatting | bytes 921600
  68.2 0.6 fusion
  (1 shorter events, 0.0 us)
